TPU v7x, 32 devices: a whole 2x2x4 slice. The times are simulated.
32 devices in a mesh: region: 8 (over z, x), batch: 4 (over y, core).
Axes of the slice: x: 2, y: 2, z: 4, core: 2. Of those that a mesh axis runs over, the one named last changes fastest.
Arguments:
- features: bfloat16 [8, 63, 32768], P('region', None, 'batch'), may hold values from -1 to 1
- spacing: float32 [8, 32768], P('region', 'batch'), may hold values from 0.000546875 to 0.59375
- counts: int32 [8, 512], P('region', 'batch'), may hold values from 0 to 64, as said below
- depth_rank: int32 [512, 8], P('batch'), may hold values from 0 to 7, each once within a row
- target: float32 [3, 512], P(None, 'batch'), may hold values from 0 to 1
- w_in: float32 [8, 64, 256], P('region', 'batch'), may hold values from -0.75 to 0.75
- w_hid: float32 [8, 2, 256, 256], P('region', None, 'batch'), may hold values from -0.375 to 0.375
- b_hid: float32 [8, 2, 256], P('region', None, 'batch'), may hold values from -1.2 to 1.2
- w_out: float32 [8, 4, 256], P('region', None, 'batch'), may hold values from -0.375 to 0.375
- mom_in: float32 [2, 8, 64, 256], P(None, 'region', 'batch'), may hold values from -1 to 4, as said below
- mom_hid: float32 [2, 8, 2, 256, 256], P(None, 'region', None, 'batch'), may hold values from -1 to 4, as said below
- mom_bias: float32 [2, 8, 2, 256], P(None, 'region', None, 'batch'), may hold values from -1 to 4, as said below
- mom_out: float32 [2, 8, 4, 256], P(None, 'region', None, 'batch'), may hold values from -1 to 4, as said below
Outputs:
- new_w_in: float32 [8, 64, 256], P('region')
- new_w_hid: float32 [8, 2, 256, 256], P('region')
- new_b_hid: float32 [8, 2, 256], P('region')
- new_w_out: float32 [8, 4, 256], P('region')
- new_mom_in: float32 [2, 8, 64, 256], P(None, 'region', 'batch')
- new_mom_hid: float32 [2, 8, 2, 256, 256], P(None, 'region', None, 'batch')
- new_mom_bias: float32 [2, 8, 2, 256], P(None, 'region', None, 'batch')
- new_mom_out: float32 [2, 8, 4, 256], P(None, 'region', None, 'batch')
Inputs may be any that keep to these rules, and one draw needn't show every extreme that they name: The first counts[c, ray] slots of a segment are live. `mom_in`: slice 0 is the first moment, slice 1 the second moment, which lies between 0.1 and 4. `mom_hid`: as for mom_in. `mom_bias`: as for mom_in. `mom_out`: as for mom_in.
All inputs are finite; a program needn't handle non-finite values.
Results may differ from a plain program's by a relative error of at most 0.012.
The roundings to bfloat16 on the way count: a program that leaves them out, or rounds other values in their place, can miss the bound.
Values may be sent and summed in bfloat16 or wider, within the bound.
A program may use at most 128 MiB of HBM per device.

v0:
```python
import functools

import jax
import jax.numpy as jnp
from jax import lax
from jax.experimental import pallas as pl
from jax.experimental.pallas import tpu as pltpu
from jax.sharding import PartitionSpec as P

MESH = pl.DeviceIdType.MESH
F32 = jnp.float32
BF16 = jnp.bfloat16
LANES = 128
ONES = 16

beta_first = 0.9
beta_second = 0.95
learn_rate = 0.01
norm_eps = 1e-06
adam_eps = 1e-08


def exact_dot(left, right):
    return jnp.dot(left, right, precision=lax.Precision.HIGHEST, preferred_element_type=F32)


def dot_nt(left, right, precision=None):
    return lax.dot_general(
        left, right, (((1,), (1,)), ((), ())), precision=precision, preferred_element_type=F32
    )


def iota(shape, axis):
    return lax.broadcasted_iota(jnp.int32, shape, axis)


def flip(index, bit):
    return index + bit - 2 * bit * ((index // bit) % 2)


def place_of(row, rows_hid, hid):
    return (iota((rows_hid, hid), 1) == iota((rows_hid, hid), 0) + row * rows_hid).astype(F32)


def kernel(
    cfg,
    feat_hbm, gaps_hbm, counts_hbm, ranks_hbm, target_hbm,
    w_in_hbm, w_hid_hbm, b_hid_hbm, w_out_hbm,
    m_in_hbm, m_hid_hbm, m_bias_hbm, m_out_hbm,
    t1, t2, t3, big,
    feat_raw, gaps_ref, counts_ref, ranks_ref, target_ref,
    w_in_ref, w_hid_ref, b_hid_ref, w_out_ref,
    m_in_ref, m_hid_ref, m_bias_ref, m_out_ref,
    feat, act1, act2, act3, back2, heads, gheads, table,
    w1b, w2b, w3b, w1t, w2t, w3t, wot, early,
    g1, g2, g3, acco, r1, r2, s1, s2, y1, y2, d3,
    in_sem, wsend, wrecv, bsend, brecv, tsend, trecv, gsend, grecv, dsend, drecv,
):
    nbatch, nregion, slots, halves, chunk = cfg
    cell = lax.axis_index("region")
    row = lax.axis_index("batch")
    enc, samples = feat_raw.shape
    hid = w2b.shape[0]
    rows_in, rows_hid = w_in_ref.shape[0], w_hid_ref.shape[1]
    block = rows_in + 2 * rows_hid + 8
    part = samples // halves
    grid = part // LANES
    per_row = LANES // slots
    full_in = feat.shape[0]

    barrier = pltpu.get_barrier_semaphore()
    for k in range(1, nbatch):
        pl.semaphore_signal(
            barrier, inc=1, device_id={"batch": lax.rem(row + k, nbatch)}, device_id_type=MESH
        )
    for k in range(1, nregion):
        pl.semaphore_signal(
            barrier, inc=1, device_id={"region": lax.rem(cell + k, nregion)}, device_id_type=MESH
        )

    origins = (
        w_in_hbm, w_out_hbm, b_hid_hbm, w_hid_hbm, feat_hbm, m_out_hbm, m_bias_hbm, m_in_hbm,
        m_hid_hbm, gaps_hbm, counts_hbm, ranks_hbm, target_hbm,
    )
    landings = (
        w_in_ref, w_out_ref, b_hid_ref, w_hid_ref, feat_raw, m_out_ref, m_bias_ref, m_in_ref,
        m_hid_ref, gaps_ref, counts_ref, ranks_ref, target_ref,
    )
    arrivals = [
        pltpu.make_async_copy(src, dst, in_sem.at[i])
        for i, (src, dst) in enumerate(zip(origins, landings))
    ]
    for arrival in arrivals:
        arrival.start()
    act1[hid:hid + ONES, :] = jnp.ones((ONES, samples), BF16)
    act2[hid:hid + ONES, :] = jnp.ones((ONES, samples), BF16)
    gheads[...] = jnp.zeros_like(gheads)
    g1[...] = jnp.zeros_like(g1)
    g2[...] = jnp.zeros_like(g2)
    g3[...] = jnp.zeros_like(g3)
    acco[...] = jnp.zeros_like(acco)
    for arrival in arrivals:
        arrival.wait()

    w1b[pl.ds(row * rows_in, rows_in), :] = w_in_ref[...].astype(BF16)
    w2b[pl.ds(row * rows_hid, rows_hid), :] = w_hid_ref[0].astype(BF16)
    w3b[pl.ds(row * rows_hid, rows_hid), :] = w_hid_ref[1].astype(BF16)
    place = place_of(row, rows_hid, hid)

    def spread(narrow_out, narrow_bias):
        narrow = jnp.concatenate(
            [narrow_out, narrow_bias, jnp.zeros((2, rows_hid), F32)], axis=0
        )
        return exact_dot(narrow, place)

    own_small = spread(w_out_ref[...], b_hid_ref[...])
    early[row] = own_small
    big[row, 0, 0:rows_in] = w_in_ref[...]
    big[row, 0, rows_in:rows_in + rows_hid] = w_hid_ref[0]
    big[row, 0, rows_in + rows_hid:rows_in + 2 * rows_hid] = w_hid_ref[1]
    big[row, 0, rows_in + 2 * rows_hid:block] = own_small
    for kind in range(2):
        big[row, kind + 1, 0:rows_in] = m_in_ref[kind]
        big[row, kind + 1, rows_in:rows_in + rows_hid] = m_hid_ref[kind, 0]
        big[row, kind + 1, rows_in + rows_hid:rows_in + 2 * rows_hid] = m_hid_ref[kind, 1]
        big[row, kind + 1, rows_in + 2 * rows_hid:block] = spread(m_out_ref[kind], m_bias_ref[kind])

    @pl.loop(0, samples // chunk)
    def _(step):
        span = pl.ds(pl.multiple_of(step * chunk, chunk), chunk)
        wide = feat_raw[:, span].astype(F32)
        feat[:, span] = jnp.concatenate([wide, jnp.ones((1, chunk), F32)], axis=0).astype(BF16)

    pl.semaphore_wait(barrier, nbatch - 1 + nregion - 1)

    pieces = (
        lambda d: w1b.at[pl.ds(d * rows_in, rows_in), :],
        lambda d: early.at[d],
        lambda d: w2b.at[pl.ds(d * rows_hid, rows_hid), :],
        lambda d: w3b.at[pl.ds(d * rows_hid, rows_hid), :],
    )

    def weight_copy(piece, k, origin, target):
        ref = pieces[piece](origin)
        return pltpu.make_async_remote_copy(
            src_ref=ref, dst_ref=ref, send_sem=wsend.at[piece, k], recv_sem=wrecv.at[piece, k],
            device_id={"batch": target}, device_id_type=MESH,
        )

    for piece in (0, 2, 1, 3):
        for k in range(1, nbatch):
            weight_copy(piece, k, row, lax.rem(row + k, nbatch)).start()

    def await_weights(piece):
        for k in range(1, nbatch):
            weight_copy(piece, k, lax.rem(row + nbatch - k, nbatch), row).wait_recv()

    bits = []
    while (1 << len(bits)) < nbatch:
        bits.append(1 << len(bits))
    high = bits[::-1]
    blocks = {}
    count = 0
    known = [0]
    for bit in high:
        blocks[bit] = []
        for held in known:
            blocks[bit].append((held, count))
            count += 1
        known = known + [held ^ bit for held in known]

    def offset(index, mask):
        for bit in bits:
            if mask & bit:
                index = flip(index, bit)
        return index

    def block_copy(bit, held, sem, incoming):
        ref = big.at[offset(row, held ^ bit if incoming else held)]
        return pltpu.make_async_remote_copy(
            src_ref=ref, dst_ref=ref, send_sem=bsend.at[sem], recv_sem=brecv.at[sem],
            device_id={"batch": flip(row, bit)}, device_id_type=MESH,
        )

    for bit in high:
        for held, sem in blocks[bit]:
            if held == 0:
                block_copy(bit, held, sem, False).start()

    square = (LANES, LANES)
    first_lane, second_lane = iota(square, 0), iota(square, 1)
    same = first_lane // slots == second_lane // slots
    upto = (same & (first_lane <= second_lane)).astype(F32)
    beyond = (same & (first_lane > second_lane)).astype(F32)
    to_ray = (first_lane // slots == second_lane % per_row).astype(F32)
    to_slot = (first_lane % per_row == second_lane // slots).astype(F32)
    ranks = ranks_ref[...].astype(F32)
    await_weights(0)
    w1t[...] = w1b[...].astype(F32).T.astype(BF16)

    def over(half, body):
        @pl.loop(0, part // chunk)
        def _(step):
            body(pl.ds(pl.multiple_of(half * part + step * chunk, chunk), chunk), step)

    def first(span, step):
        pre = jnp.dot(w1t[...], feat[:, span], preferred_element_type=F32)
        act1[0:hid, span] = jnp.maximum(pre, 0.0).astype(BF16)

    for half in range(halves):
        over(half, first)
    await_weights(1)
    small = early[0]
    for d in range(1, nbatch):
        small = small + early[d]
    wide_out = small.astype(BF16)
    tall = small.T
    wot[...] = tall.astype(BF16)
    bias_two, bias_three = tall[:, 4:5], tall[:, 5:6]

    def forward(half):
        def second(span, step):
            pre = jnp.dot(w2t[...], act1[0:hid, span], preferred_element_type=F32) + bias_two
            act2[0:hid, span] = jnp.maximum(pre, 0.0).astype(BF16)

        def third(span, step):
            pre = jnp.dot(w3t[...], act2[0:hid, span], preferred_element_type=F32) + bias_three
            act = jnp.maximum(pre, 0.0).astype(BF16)
            act3[:, span] = act
            out = jnp.dot(wide_out, act, preferred_element_type=F32)
            for t in range(chunk // LANES):
                at = half * grid * 8 + step * (chunk // LANES * 8) + t * 8
                heads[pl.ds(pl.multiple_of(at, 8), 8), :] = out[:, t * LANES:(t + 1) * LANES]

        if half == 0:
            await_weights(2)
            w2t[...] = w2b[...].astype(F32).T.astype(BF16)
        over(half, second)
        if half == 0:
            await_weights(3)
            w3t[...] = w3b[...].astype(F32).T.astype(BF16)
        over(half, third)

    def optical(half):
        raw = [heads[pl.ds(half * grid * 8 + k, grid, stride=8), :] for k in range(4)]
        gaps = gaps_ref[half * grid:(half + 1) * grid, :]
        lane, line = iota((grid, LANES), 1), iota((grid, LANES), 0)
        mine = lane // per_row == line + half * grid
        counted = exact_dot(jnp.where(mine, counts_ref[...].astype(F32), 0.0), to_slot)
        live = ((lane % slots).astype(F32) < counted - 0.5).astype(F32)
        softplus = jnp.maximum(raw[0], 0.0) + jnp.log1p(jnp.exp(-jnp.abs(raw[0])))
        depth = softplus * gaps * live
        shade = [jax.nn.sigmoid(raw[k]) for k in (1, 2, 3)]
        cum_in = exact_dot(depth, upto)
        series = depth * (1.0 - depth * (0.5 - depth * (1.0 / 6.0 - depth * (1.0 / 24.0))))
        opacity = jnp.where(depth < 0.02, series, 1.0 - jnp.exp(-depth))
        weight = jnp.exp(-(cum_in - depth)) * opacity
        stacked = jnp.concatenate([weight * shade[k] for k in range(3)] + [-depth], axis=0)
        gathered = exact_dot(stacked, to_ray)
        lines = [
            jnp.sum(
                jnp.where(mine, gathered[k * grid:(k + 1) * grid], 0.0), axis=0, keepdims=True
            )
            for k in range(4)
        ]
        table[half, cell] = jnp.concatenate(lines + [jnp.zeros((4, LANES), F32)], axis=0)
        return mine, gaps, live, raw[0], shade, cum_in, weight

    def table_copy(half, k, origin, target):
        ref = table.at[half, origin]
        return pltpu.make_async_remote_copy(
            src_ref=ref, dst_ref=ref, send_sem=tsend.at[half, k], recv_sem=trecv.at[half, k],
            device_id={"region": target}, device_id_type=MESH,
        )

    def composite(half, kept):
        mine, gaps, live, raw, shade, cum_in, weight = kept
        every = [table[half, :, k, :] for k in range(4)]
        prefix = jnp.zeros((nregion, LANES), F32)
        for j in range(nregion):
            prefix = prefix + jnp.where(ranks[j:j + 1] < ranks, every[3][j:j + 1], 0.0)
        reach = jnp.exp(prefix)
        here = iota((nregion, LANES), 0) == cell
        own_rank = jnp.sum(jnp.where(here, ranks, 0.0), axis=0, keepdims=True)
        own_reach = jnp.sum(jnp.where(here, reach, 0.0), axis=0, keepdims=True)
        later = ranks > own_rank
        grad_log = jnp.zeros((1, LANES), F32)
        per_ray = []
        for k in range(3):
            lit = reach * every[k]
            grad_colour = 2.0 * (jnp.sum(lit, axis=0, keepdims=True) - target_ref[k:k + 1])
            behind = jnp.sum(jnp.where(later, lit, 0.0), axis=0, keepdims=True)
            grad_log = grad_log + grad_colour * behind
            per_ray.append(own_reach * grad_colour)
        stacked = jnp.concatenate(
            [jnp.where(mine, x, 0.0) for x in per_ray + [grad_log]], axis=0
        )
        laid = exact_dot(stacked, to_slot)
        grad_seg = [laid[k * grid:(k + 1) * grid] for k in range(3)]
        emit = grad_seg[0] * shade[0] + grad_seg[1] * shade[1] + grad_seg[2] * shade[2]
        after = exact_dot(emit * weight, beyond)
        grad_depth = emit * jnp.exp(-cum_in) - after - laid[3 * grid:4 * grid]
        base = half * grid * 8
        gheads[pl.ds(base, grid, stride=8), :] = grad_depth * live * gaps * jax.nn.sigmoid(raw)
        for k in range(3):
            gheads[pl.ds(base + k + 1, grid, stride=8), :] = (
                grad_seg[k] * weight * shade[k] * (1.0 - shade[k])
            )

    def backward_three(half):
        def body(span, step):
            tiles = []
            for t in range(chunk // LANES):
                at = half * grid * 8 + step * (chunk // LANES * 8) + t * 8
                tiles.append(gheads[pl.ds(pl.multiple_of(at, 8), 8), :])
            grad_heads = jnp.concatenate(tiles, axis=1).astype(BF16)
            act = act3[:, span]
            acco[...] += dot_nt(grad_heads, act)
            raw = jnp.dot(wot[...], grad_heads, preferred_element_type=F32).astype(BF16)
            back3 = jnp.where(act > 0, raw, jnp.zeros_like(raw))
            g1[...] += dot_nt(act2[:, span], back3)
            raw = jnp.dot(w3b[...], back3, preferred_element_type=F32).astype(BF16)
            back2[:, span] = jnp.where(act2[0:hid, span] > 0, raw, jnp.zeros_like(raw))

        over(half, body)

    def grad_two(half):
        def body(span, step):
            g2[...] += dot_nt(act1[:, span], back2[:, span])

        over(half, body)

    def backward_one(half):
        def body(span, step):
            raw = jnp.dot(w2b[...], back2[:, span], preferred_element_type=F32).astype(BF16)
            back1 = jnp.where(act1[0:hid, span] > 0, raw, jnp.zeros_like(raw))
            g3[...] += dot_nt(feat[:, span], back1)

        over(half, body)

    kept = []
    for half in range(halves):
        forward(half)
        kept.append(optical(half))
        for k in range(1, nregion):
            table_copy(half, k, cell, lax.rem(cell + k, nregion)).start()
    for half in range(halves):
        for k in range(1, nregion):
            table_copy(half, k, lax.rem(cell + nregion - k, nregion), cell).wait_recv()
        composite(half, kept[half])
        backward_three(half)

    side = row % 2
    partner = flip(row, 1)

    def grad_copy(src, dst, sem, target):
        return pltpu.make_async_remote_copy(
            src_ref=src, dst_ref=dst, send_sem=gsend.at[sem], recv_sem=grecv.at[sem],
            device_id={"batch": target}, device_id_type=MESH,
        )

    steps = 2 + len(bits) - 1

    def reduce_start(group, g, r):
        length = r.shape[0]
        away = g.at[pl.ds(pl.multiple_of((1 - side) * length, 8), length), :]
        copy = grad_copy(away, r, group * steps, partner)
        copy.start()
        return copy

    def reduce_across(group, g, r, s, y, copy):
        length = r.shape[0]
        copy.wait_recv()
        near = g[pl.ds(pl.multiple_of(side * length, 8), length), :]
        s[0] = (near + r[...]).astype(BF16)
        return [
            grad_copy(s.at[i], y.at[i], group * steps + 1 + i, flip(row, bit))
            for i, bit in enumerate(bits[1:])
        ]

    def reduce_stages(group, s, y, t, copies):
        length = s.shape[1]
        for i, copy in enumerate(copies):
            if i > 0:
                s[i] = total.astype(BF16)
                copy.start()
            copy.wait_recv()
            total = s[i].astype(F32) + y[i].astype(F32)
        span = pl.ds(pl.multiple_of(side * length, 8), length)
        t[span, :] = total
        last = grad_copy(t.at[span, :], t.at[span, :], group * steps + steps - 1, partner)
        last.start()
        return last

    def reduce_end(group, t):
        length = t.shape[0] // 2
        span = pl.ds(pl.multiple_of((1 - side) * length, 8), length)
        grad_copy(t.at[span, :], t.at[span, :], group * steps + steps - 1, partner).wait_recv()

    g1[hid + 8:hid + ONES, :] = acco[...]
    first_one = reduce_start(0, g1, r1)
    grad_two(0)
    cross_one = reduce_across(0, g1, r1, s1, y1, first_one)
    for copy in cross_one[:1]:
        copy.start()
    for half in range(1, halves):
        grad_two(half)
    first_two = reduce_start(1, g2, r2)
    for bit in high[:-1]:
        for held, sem in blocks[bit]:
            block_copy(bit, held, sem, True).wait_recv()
    for held, sem in blocks[high[-1]]:
        if held != 0:
            block_copy(high[-1], held, sem, False).start()
    backward_one(0)
    last_one = reduce_stages(0, s1, y1, t1, cross_one)
    cross_two = reduce_across(1, g2, r2, s2, y2, first_two)
    for copy in cross_two[:1]:
        copy.start()
    for half in range(1, halves):
        backward_one(half)

    d3[row] = g3[...].astype(BF16)

    def direct_copy(k, origin, target):
        return pltpu.make_async_remote_copy(
            src_ref=d3.at[origin], dst_ref=d3.at[origin], send_sem=dsend.at[k],
            recv_sem=drecv.at[k], device_id={"batch": target}, device_id_type=MESH,
        )

    for k in range(1, nbatch):
        direct_copy(k, row, lax.rem(row + k, nbatch)).start()
    last_two = reduce_stages(1, s2, y2, t2, cross_two)
    for k in range(1, nbatch):
        direct_copy(k, lax.rem(row + nbatch - k, nbatch), row).wait_recv()
    total = d3[0].astype(F32)
    for d in range(1, nbatch):
        total = total + d3[d].astype(F32)
    t3[...] = total
    reduce_end(0, t1)
    for held, sem in blocks[high[-1]]:
        block_copy(high[-1], held, sem, True).wait_recv()
    reduce_end(1, t2)

    for piece in range(4):
        for k in range(1, nbatch):
            weight_copy(piece, k, row, lax.rem(row + k, nbatch)).wait_send()
    for bit in high:
        for held, sem in blocks[bit]:
            block_copy(bit, held, sem, False).wait_send()
    for half in range(halves):
        for k in range(1, nregion):
            table_copy(half, k, cell, lax.rem(cell + k, nregion)).wait_send()
    for k in range(1, nbatch):
        direct_copy(k, row, lax.rem(row + k, nbatch)).wait_send()
    for copy in [first_one, first_two, last_one, last_two] + cross_one + cross_two:
        copy.wait_send()


def step_kernel(
    cfg, t1, t2, t3, big, nw_in, nw_hid, nb_hid, nw_out, nm_in, nm_hid, nm_bias, nm_out
):
    nbatch, rows_in, rows_hid = cfg
    row = lax.axis_index("batch")
    full_in, hid = nw_in.shape
    block = big.shape[2]
    place = place_of(row, rows_hid, hid)
    count_all = full_in * hid + 2 * hid * hid + 6 * hid
    last_rows = jnp.concatenate(
        [t1[hid + 8:hid + 12, :], t2[hid:hid + 1, :], t1[hid:hid + 1, :], jnp.zeros((2, hid), F32)],
        axis=0,
    )

    def squares(x):
        return jnp.sum(x * x, axis=0, keepdims=True)

    columns = (
        squares(t1[0:hid, :]) + squares(t2[0:hid, :]) + squares(t3[...])
        + squares(last_rows)
    )
    total_sq = jnp.sum(columns, axis=1, keepdims=True)
    scale = lax.rsqrt(total_sq / count_all + norm_eps)

    def adam(grad, param, first, second):
        scaled = grad * scale
        first = beta_first * first + (1.0 - beta_first) * scaled
        second = beta_second * second + (1.0 - beta_second) * scaled * scaled
        return param - learn_rate * first / (jnp.sqrt(second) + adam_eps), first, second

    def span_of(d, rows, start=0):
        return pl.ds(pl.multiple_of(start + d * rows, 8), rows)

    def update(d, grad, lo, rows):
        return adam(
            grad, big[d, 0, lo:lo + rows], big[d, 1, lo:lo + rows], big[d, 2, lo:lo + rows]
        )

    lo_two, lo_three, lo_small = rows_in, rows_in + rows_hid, rows_in + 2 * rows_hid
    for d in range(nbatch):
        at_in = slice(d * rows_in, (d + 1) * rows_in)
        at_hid = slice(d * rows_hid, (d + 1) * rows_hid)
        nw_in[at_in, :] = update(d, t3[at_in, :], 0, rows_in)[0]
        nw_hid[0, at_hid, :] = update(d, t2[at_hid, :], lo_two, rows_hid)[0]
        nw_hid[1, at_hid, :] = update(d, t1[at_hid, :], lo_three, rows_hid)[0]
    whole = []
    for kind in range(3):
        value = big[0, kind, lo_small:block]
        for d in range(1, nbatch):
            value = value + big[d, kind, lo_small:block]
        whole.append(value)
    fresh, first, second = adam(last_rows, *whole)
    nw_out[...] = fresh[0:4]
    nb_hid[...] = fresh[4:6]
    for kind, value in enumerate((first, second)):
        narrow = dot_nt(value, place, lax.Precision.HIGHEST)
        nm_out[kind] = narrow[0:4]
        nm_bias[kind] = narrow[4:6]
    _, first, second = update(row, t3[span_of(row, rows_in), :], 0, rows_in)
    nm_in[0], nm_in[1] = first, second
    _, first, second = update(row, t2[span_of(row, rows_hid), :], lo_two, rows_hid)
    nm_hid[0, 0], nm_hid[1, 0] = first, second
    _, first, second = update(row, t1[span_of(row, rows_hid), :], lo_three, rows_hid)
    nm_hid[0, 1], nm_hid[1, 1] = first, second


def body(
    features, spacing, counts, depth_rank, target, w_in, w_hid, b_hid, w_out,
    mom_in, mom_hid, mom_bias, mom_out,
):
    nbatch, nregion = lax.axis_size("batch"), lax.axis_size("region")
    _, enc, samples = features.shape
    rays = counts.shape[1]
    slots = samples // rays
    hid = w_in.shape[2]
    rows_in, rows_hid = w_in.shape[1], w_hid.shape[2]
    full_in = rows_in * nbatch
    halves = 2
    chunk = min(2048, samples // halves)
    block = rows_in + 2 * rows_hid + 8
    levels = nbatch.bit_length() - 1
    len1 = (hid + ONES) // 2
    len2 = len1
    cfg = (nbatch, nregion, slots, halves, chunk)
    vmem = pl.BlockSpec(memory_space=pltpu.VMEM)
    shape = lambda *dims: jax.ShapeDtypeStruct(dims, F32)
    dma = pltpu.SemaphoreType.DMA
    crossing = max(levels - 1, 1)
    sums = pl.pallas_call(
        functools.partial(kernel, cfg),
        out_shape=(
            pltpu.VMEM((2 * len1, hid), F32), pltpu.VMEM((2 * len2, hid), F32),
            pltpu.VMEM((full_in, hid), F32), pltpu.VMEM((nbatch, 3, block, hid), F32),
        ),
        in_specs=[pl.BlockSpec(memory_space=pltpu.HBM)] * 13,
        out_specs=(vmem,) * 4,
        scratch_shapes=[
            pltpu.VMEM((enc, samples), BF16),
            pltpu.VMEM((samples // LANES, LANES), F32),
            pltpu.VMEM(counts.shape, jnp.int32),
            pltpu.VMEM((nregion, rays), jnp.int32),
            pltpu.VMEM(target.shape, F32),
            pltpu.VMEM(w_in.shape[1:], F32),
            pltpu.VMEM(w_hid.shape[1:], F32),
            pltpu.VMEM(b_hid.shape[1:], F32),
            pltpu.VMEM(w_out.shape[1:], F32),
            pltpu.VMEM((2,) + mom_in.shape[2:], F32),
            pltpu.VMEM((2,) + mom_hid.shape[2:], F32),
            pltpu.VMEM((2,) + mom_bias.shape[2:], F32),
            pltpu.VMEM((2,) + mom_out.shape[2:], F32),
            pltpu.VMEM((full_in, samples), BF16),
            pltpu.VMEM((hid + ONES, samples), BF16),
            pltpu.VMEM((hid + ONES, samples), BF16),
            pltpu.VMEM((hid, samples), BF16),
            pltpu.VMEM((hid, samples), BF16),
            pltpu.VMEM((samples // LANES * 8, LANES), F32),
            pltpu.VMEM((samples // LANES * 8, LANES), F32),
            pltpu.VMEM((halves, nregion, 8, LANES), F32),
            pltpu.VMEM((full_in, hid), BF16),
            pltpu.VMEM((hid, hid), BF16),
            pltpu.VMEM((hid, hid), BF16),
            pltpu.VMEM((hid, full_in), BF16),
            pltpu.VMEM((hid, hid), BF16),
            pltpu.VMEM((hid, hid), BF16),
            pltpu.VMEM((hid, 8), BF16),
            pltpu.VMEM((nbatch, 8, hid), F32),
            pltpu.VMEM((2 * len1, hid), F32),
            pltpu.VMEM((2 * len2, hid), F32),
            pltpu.VMEM((full_in, hid), F32),
            pltpu.VMEM((8, hid), F32),
            pltpu.VMEM((len1, hid), F32),
            pltpu.VMEM((len2, hid), F32),
            pltpu.VMEM((crossing, len1, hid), BF16),
            pltpu.VMEM((crossing, len2, hid), BF16),
            pltpu.VMEM((crossing, len1, hid), BF16),
            pltpu.VMEM((crossing, len2, hid), BF16),
            pltpu.VMEM((nbatch, full_in, hid), BF16),
            dma((13,)),
            dma((4, nbatch)),
            dma((4, nbatch)),
            dma((nbatch,)),
            dma((nbatch,)),
            dma((halves, nregion)),
            dma((halves, nregion)),
            dma((2 * (levels + 1),)),
            dma((2 * (levels + 1),)),
            dma((nbatch,)),
            dma((nbatch,)),
        ],
        compiler_params=pltpu.CompilerParams(
            collective_id=0, has_side_effects=True, vmem_limit_bytes=44 * 1024 * 1024
        ),
        name="window",
    )(*[
        pltpu.with_memory_space_constraint(x, pltpu.HBM) for x in (
            features[0], spacing.reshape(samples // LANES, LANES), counts, depth_rank.T, target,
            w_in[0], w_hid[0], b_hid[0], w_out[0],
            mom_in[:, 0], mom_hid[:, 0], mom_bias[:, 0], mom_out[:, 0],
        )
    ])
    outs = pl.pallas_call(
        functools.partial(step_kernel, (nbatch, rows_in, rows_hid)),
        out_shape=(
            shape(full_in, hid), shape(2, hid, hid), shape(2, hid), shape(4, hid),
            shape(2, rows_in, hid), shape(2, 2, rows_hid, hid),
            shape(2, 2, rows_hid), shape(2, 4, rows_hid),
        ),
        in_specs=[vmem] * 4,
        out_specs=(vmem,) * 8,
        compiler_params=pltpu.CompilerParams(vmem_limit_bytes=16 * 1024 * 1024),
        name="step",
    )(*sums)
    return tuple(x[None] for x in outs[:4]) + tuple(x[:, None] for x in outs[4:])


def solution(mesh):
    return jax.shard_map(
        body,
        mesh=mesh,
        in_specs=(
            P("region", None, "batch"),
            P("region", "batch"),
            P("region", "batch"),
            P("batch", None),
            P(None, "batch"),
            P("region", "batch", None),
            P("region", None, "batch", None),
            P("region", None, "batch"),
            P("region", None, "batch"),
            P(None, "region", "batch", None),
            P(None, "region", None, "batch", None),
            P(None, "region", None, "batch"),
            P(None, "region", None, "batch"),
        ),
        out_specs=(
            P("region", None, None),
            P("region", None, None, None),
            P("region", None, None),
            P("region", None, None),
            P(None, "region", "batch", None),
            P(None, "region", None, "batch", None),
            P(None, "region", None, "batch"),
            P(None, "region", None, "batch"),
        ),
        check_vma=False,
    )
```

profile of v0, /device:TPU:0, one launch (start us, length us, event | category | flops | bytes accessed | tf_op | source)
XLA Modules:
  0.0 35.7 jit_solution(1561192260540122655)
XLA Ops:
  0.6 33.7 %window.1 = (f32[272,256]{1,0:T(8,128)S(1)}, f32[272,256]{1,0:T(8,128)S(1)}, f32[64,256]{1,0:T(8,128)S(1)}, f32[4,3,152,256]{3,2,1,0:T(8,128)S(1)}) custom-call(bf16[63,8192]{1,0:T(8,128)(2,1)} %bitcast.27, f32[64,128]{1,0:T(8,128)} %bitcast.30, s32[1,128]{1,0:T(1,128)} %counts_hbm.1, s32[8,128]{1,0:T(8,128)} %bitcast.33, f32[3,128]{1,0:T(4,128)} %target_hbm.1, ...), custom_call_target="tpu_custom_call" | custom-call | tf_op jit(solution)/shard_map/window/pallas_call | solution.py:548
  34.4 1.4 %step.1 = (f32[64,256]{1,0:T(8,128)}, f32[2,256,256]{2,1,0:T(8,128)}, f32[2,256]{1,0:T(2,128)}, f32[4,256]{1,0:T(4,128)}, f32[2,16,256]{2,1,0:T(8,128)}, /*index...) custom-call(f32[272,256]{1,0:T(8,128)S(1)} %get-tuple-element.20.t1, ...), custom_call_target="tpu_custom_call" | custom-call | tf_op jit(solution)/shard_map/step/pallas_call | solution.py:620
where the time goes:
time: 36 us; the launch traced here: 35.7 us
  Pallas kernels  35.1 us (98%)
  between operations  0.65 us (2%)
    pallas_call x1, Pallas kernels, body(): pl.pallas_call(functools.partial(kernel, cfg), out_shape=(pltpu.VMEM((2 *...  33.7 us
    pallas_call x1, Pallas kernels, body(): pl.pallas_call(functools.partial(step_kernel, (nbatch, rows_in, rows_hid)...  1.38 us

commit v1 on v0

--- a/solution.py
+++ b/solution.py
@@ -53,7 +53,7 @@
     m_in_ref, m_hid_ref, m_bias_ref, m_out_ref,
     feat, act1, act2, act3, back2, heads, gheads, table,
     w1b, w2b, w3b, w1t, w2t, w3t, wot, early,
-    g1, g2, g3, acco, r1, r2, s1, s2, y1, y2, d3,
+    g1, g2, g3, acco, r1, r2, s1, s2, y1, y2, z1, z2, d3,
     in_sem, wsend, wrecv, bsend, brecv, tsend, trecv, gsend, grecv, dsend, drecv,
 ):
     nbatch, nregion, slots, halves, chunk = cfg
@@ -378,7 +378,7 @@
             for i, bit in enumerate(bits[1:])
         ]
 
-    def reduce_stages(group, s, y, t, copies):
+    def reduce_stages(group, s, y, t, z, copies):
         length = s.shape[1]
         for i, copy in enumerate(copies):
             if i > 0:
@@ -387,23 +387,28 @@
             copy.wait_recv()
             total = s[i].astype(F32) + y[i].astype(F32)
         span = pl.ds(pl.multiple_of(side * length, 8), length)
-        t[span, :] = total
-        last = grad_copy(t.at[span, :], t.at[span, :], group * steps + steps - 1, partner)
+        z[side] = total.astype(BF16)
+        t[span, :] = total.astype(BF16).astype(F32)
+        last = grad_copy(z.at[side], z.at[side], group * steps + steps - 1, partner)
         last.start()
         return last
 
-    def reduce_end(group, t):
+    def reduce_end(group, t, z):
         length = t.shape[0] // 2
         span = pl.ds(pl.multiple_of((1 - side) * length, 8), length)
-        grad_copy(t.at[span, :], t.at[span, :], group * steps + steps - 1, partner).wait_recv()
-
+        there = z.at[1 - side]
+        grad_copy(there, there, group * steps + steps - 1, partner).wait_recv()
+        t[span, :] = z[1 - side].astype(F32)
+
+    middle = halves // 2
     g1[hid + 8:hid + ONES, :] = acco[...]
     first_one = reduce_start(0, g1, r1)
-    grad_two(0)
+    for half in range(middle):
+        grad_two(half)
     cross_one = reduce_across(0, g1, r1, s1, y1, first_one)
     for copy in cross_one[:1]:
         copy.start()
-    for half in range(1, halves):
+    for half in range(middle, halves):
         grad_two(half)
     first_two = reduce_start(1, g2, r2)
     for bit in high[:-1]:
@@ -413,7 +418,6 @@
         if held != 0:
             block_copy(high[-1], held, sem, False).start()
     backward_one(0)
-    last_one = reduce_stages(0, s1, y1, t1, cross_one)
     cross_two = reduce_across(1, g2, r2, s2, y2, first_two)
     for copy in cross_two[:1]:
         copy.start()
@@ -430,17 +434,18 @@
 
     for k in range(1, nbatch):
         direct_copy(k, row, lax.rem(row + k, nbatch)).start()
-    last_two = reduce_stages(1, s2, y2, t2, cross_two)
+    last_one = reduce_stages(0, s1, y1, t1, z1, cross_one)
+    last_two = reduce_stages(1, s2, y2, t2, z2, cross_two)
     for k in range(1, nbatch):
         direct_copy(k, lax.rem(row + nbatch - k, nbatch), row).wait_recv()
     total = d3[0].astype(F32)
     for d in range(1, nbatch):
         total = total + d3[d].astype(F32)
     t3[...] = total
-    reduce_end(0, t1)
+    reduce_end(0, t1, z1)
     for held, sem in blocks[high[-1]]:
         block_copy(high[-1], held, sem, True).wait_recv()
-    reduce_end(1, t2)
+    reduce_end(1, t2, z2)
 
     for piece in range(4):
         for k in range(1, nbatch):
@@ -593,6 +598,8 @@
             pltpu.VMEM((crossing, len2, hid), BF16),
             pltpu.VMEM((crossing, len1, hid), BF16),
             pltpu.VMEM((crossing, len2, hid), BF16),
+            pltpu.VMEM((2, len1, hid), BF16),
+            pltpu.VMEM((2, len2, hid), BF16),
             pltpu.VMEM((nbatch, full_in, hid), BF16),
             dma((13,)),
             dma((4, nbatch)),

time: 36 us -> 34.8 us (0.967)
  Pallas kernels: 35.1 us -> 33.9 us
    pallas_call x1, Pallas kernels: 33.7 us -> 32.5 us  [body(): pl.pallas_call(functools.partial(kernel, cfg), out_shape=(pltpu.VMEM((2 *...]
where the time goes in v1:
time: 34.8 us; the launch traced here: 34.6 us
  Pallas kernels  33.9 us (97%)
  between operations  0.65 us (2%)
    pallas_call x1, Pallas kernels, body(): pl.pallas_call(functools.partial(kernel, cfg), out_shape=(pltpu.VMEM((2 *...  32.5 us
    pallas_call x1, Pallas kernels, body(): pl.pallas_call(functools.partial(step_kernel, (nbatch, rows_in, rows_hid)...  1.38 us

profile of v1, /device:TPU:0, one launch (start us, length us, event | category | flops | bytes accessed | tf_op | source)
XLA Modules:
  0.0 34.6 jit_solution(10298813708226011639)
XLA Ops:
  0.6 32.5 %window.1 = (f32[272,256]{1,0:T(8,128)S(1)}, f32[272,256]{1,0:T(8,128)S(1)}, f32[64,256]{1,0:T(8,128)S(1)}, f32[4,3,152,256]{3,2,1,0:T(8,128)S(1)}) custom-call(bf16[63,8192]{1,0:T(8,128)(2,1)} %bitcast.27, f32[64,128]{1,0:T(8,128)} %bitcast.30, s32[1,128]{1,0:T(1,128)} %counts_hbm.1, s32[8,128]{1,0:T(8,128)} %bitcast.33, f32[3,128]{1,0:T(4,128)} %target_hbm.1, ...), custom_call_target="tpu_custom_call" | custom-call | tf_op jit(solution)/shard_map/window/pallas_call | solution.py:553
  33.2 1.4 %step.1 = (f32[64,256]{1,0:T(8,128)}, f32[2,256,256]{2,1,0:T(8,128)}, f32[2,256]{1,0:T(2,128)}, f32[4,256]{1,0:T(4,128)}, f32[2,16,256]{2,1,0:T(8,128)}, /*index...) custom-call(f32[272,256]{1,0:T(8,128)S(1)} %get-tuple-element.20.t1, ...), custom_call_target="tpu_custom_call" | custom-call | tf_op jit(solution)/shard_map/step/pallas_call | solution.py:627

commit v2 on v0

--- a/solution.py
+++ b/solution.py
@@ -263,7 +263,7 @@
             )
             for k in range(4)
         ]
-        table[half, cell] = jnp.concatenate(lines + [jnp.zeros((4, LANES), F32)], axis=0)
+        table[half, cell] = jnp.concatenate(lines, axis=0)
         return mine, gaps, live, raw[0], shade, cum_in, weight
 
     def table_copy(half, k, origin, target):
@@ -397,13 +397,15 @@
         span = pl.ds(pl.multiple_of((1 - side) * length, 8), length)
         grad_copy(t.at[span, :], t.at[span, :], group * steps + steps - 1, partner).wait_recv()
 
+    middle = halves // 2
     g1[hid + 8:hid + ONES, :] = acco[...]
     first_one = reduce_start(0, g1, r1)
-    grad_two(0)
+    for half in range(middle):
+        grad_two(half)
     cross_one = reduce_across(0, g1, r1, s1, y1, first_one)
     for copy in cross_one[:1]:
         copy.start()
-    for half in range(1, halves):
+    for half in range(middle, halves):
         grad_two(half)
     first_two = reduce_start(1, g2, r2)
     for bit in high[:-1]:
@@ -413,7 +415,6 @@
         if held != 0:
             block_copy(high[-1], held, sem, False).start()
     backward_one(0)
-    last_one = reduce_stages(0, s1, y1, t1, cross_one)
     cross_two = reduce_across(1, g2, r2, s2, y2, first_two)
     for copy in cross_two[:1]:
         copy.start()
@@ -430,6 +431,7 @@
 
     for k in range(1, nbatch):
         direct_copy(k, row, lax.rem(row + k, nbatch)).start()
+    last_one = reduce_stages(0, s1, y1, t1, cross_one)
     last_two = reduce_stages(1, s2, y2, t2, cross_two)
     for k in range(1, nbatch):
         direct_copy(k, lax.rem(row + nbatch - k, nbatch), row).wait_recv()
@@ -574,7 +576,7 @@
             pltpu.VMEM((hid, samples), BF16),
             pltpu.VMEM((samples // LANES * 8, LANES), F32),
             pltpu.VMEM((samples // LANES * 8, LANES), F32),
-            pltpu.VMEM((halves, nregion, 8, LANES), F32),
+            pltpu.VMEM((halves, nregion, 4, LANES), F32),
             pltpu.VMEM((full_in, hid), BF16),
             pltpu.VMEM((hid, hid), BF16),
             pltpu.VMEM((hid, hid), BF16),

time: 36 us -> 34.7 us (0.964)
  Pallas kernels: 35.1 us -> 33.9 us
    pallas_call x1, Pallas kernels: 33.7 us -> 32.5 us  [body(): pl.pallas_call(functools.partial(kernel, cfg), out_shape=(pltpu.VMEM((2 *...]
where the time goes in v2:
time: 34.7 us; the launch traced here: 34.5 us
  Pallas kernels  33.9 us (98%)
  between operations  0.65 us (2%)
    pallas_call x1, Pallas kernels, body(): pl.pallas_call(functools.partial(kernel, cfg), out_shape=(pltpu.VMEM((2 *...  32.5 us
    pallas_call x1, Pallas kernels, body(): pl.pallas_call(functools.partial(step_kernel, (nbatch, rows_in, rows_hid)...  1.38 us

profile of v2, /device:TPU:0, one launch (start us, length us, event | category | flops | bytes accessed | tf_op | source)
XLA Modules:
  0.0 34.5 jit_solution(12092455136067650806)
XLA Ops:
  0.6 32.5 %window.1 = (f32[272,256]{1,0:T(8,128)S(1)}, f32[272,256]{1,0:T(8,128)S(1)}, f32[64,256]{1,0:T(8,128)S(1)}, f32[4,3,152,256]{3,2,1,0:T(8,128)S(1)}) custom-call(bf16[63,8192]{1,0:T(8,128)(2,1)} %bitcast.27, f32[64,128]{1,0:T(8,128)} %bitcast.30, s32[1,128]{1,0:T(1,128)} %counts_hbm.1, s32[8,128]{1,0:T(8,128)} %bitcast.33, f32[3,128]{1,0:T(4,128)} %target_hbm.1, ...), custom_call_target="tpu_custom_call" | custom-call | tf_op jit(solution)/shard_map/window/pallas_call | solution.py:550
  33.1 1.4 %step.1 = (f32[64,256]{1,0:T(8,128)}, f32[2,256,256]{2,1,0:T(8,128)}, f32[2,256]{1,0:T(2,128)}, f32[4,256]{1,0:T(4,128)}, f32[2,16,256]{2,1,0:T(8,128)}, /*index...) custom-call(f32[272,256]{1,0:T(8,128)S(1)} %get-tuple-element.20.t1, ...), custom_call_target="tpu_custom_call" | custom-call | tf_op jit(solution)/shard_map/step/pallas_call | solution.py:622
